TPU v7x, 32 devices: a whole 2x2x4 slice. The times are simulated.
32 devices in a mesh: grp: 2 (over x), inp: 4 (over y, core), out: 4 (over z).
Axes of the slice: x: 2, y: 2, z: 4, core: 2. Of those that a mesh axis runs over, the one named last changes fastest.
Arguments:
- activations: bfloat16 [4, 512, 8192], P('grp', 'out', 'inp'), parts along dimension 0, may hold values from -6 to 6
- out_grads: bfloat16 [4, 512, 28672], P('grp', 'inp', 'out'), parts along dimension 0, may hold values from -6 to 6
- query_grads: bfloat16 [2, 28672, 8192], P(None, 'out', 'inp'), may hold values from -0.00036621094 to 0.00036621094
- token_ids: int32 [4, 512], P('grp'), parts along dimension 0, may hold values from 0 to 128255
- loss_mask: int32 [4, 512], P('grp'), parts along dimension 0, may hold values 0 or 1
Outputs:
- scores: float32 [2, 4, 512], P(None, 'grp'), parts along dimension 1
There are 2 independent parts, one for each index of `grp`. A program takes and returns all parts, laid end to end along the dimension named above; an argument that names none is the same for every part. Nothing has to cross between parts.
All inputs are finite; a program needn't handle non-finite values.
Results may differ from a plain program's by a relative error of at most 0.0003.
Values may be sent and summed in bfloat16 or wider, within the bound.
A program may use at most 128 MiB of HBM per device.

v0:
```python
import jax
import jax.numpy as jnp
from jax import lax
from jax.sharding import PartitionSpec as P


def shards(activations, out_grads, query_grads, token_ids, loss_mask):
    blocks = activations.shape[0]
    partials = []
    for number in range(blocks):
        gathered = lax.all_gather(activations[number], "out", axis=0, tiled=True)
        projected = jnp.einsum(
            "to,qoi->tqi",
            lax.all_gather(out_grads[number], "inp", axis=0, tiled=True),
            query_grads,
            preferred_element_type=jnp.float32,
        )
        partial_value = jnp.sum(projected * gathered.astype(jnp.float32)[:, None, :], axis=2)
        partial_value = lax.psum(partial_value, ("inp", "out"))
        partials.append(partial_value)
    stacked = jnp.stack(partials)
    equal = token_ids[:, :, None] == token_ids[:, None, :]
    counts = jnp.sum(equal.astype(jnp.int32), axis=2)
    weight = loss_mask.astype(jnp.float32) / counts.astype(jnp.float32)
    return jnp.transpose(stacked * weight[:, :, None], (2, 0, 1))


def solution(mesh):
    in_specs = (
        P("grp", "out", "inp"),
        P("grp", "inp", "out"),
        P(None, "out", "inp"),
        P("grp", None),
        P("grp", None),
    )
    out_specs = P(None, "grp", None)
    return jax.shard_map(shards, mesh=mesh, in_specs=in_specs, out_specs=out_specs, check_vma=False)
```

profile of v0, /device:TPU:0, one launch (start us, length us, event | category | flops | bytes accessed | tf_op | source)
XLA Modules:
  0.0 289.7 jit_solution(5545557528172188764)
XLA Ops:
  6.5 0.0 copy-start
  6.5 0.0 copy-start.1
  6.5 0.0 all-gather.15.cloned.1.call-start
  6.5 2.3 fusion.10
  8.9 0.0 all-gather.15.cloned.1.call-update
  8.9 0.0 all-gather.11.cloned.1.call-start
  8.9 0.7 all-gather.11.cloned.1.call-update
  9.6 0.0 all-gather.13.cloned.1.call-start
  9.7 4.1 %fusion.9 = (bf16[1,128,7168]{2,1,0:T(8,128)(2,1)}, bf16[1,128,7168]{2,1,0:T(8,128)(2,1)}) fusion(bf16[2,128,7168]{2,1,0:T(8,128)(2,1)} %param.6), kind=kLoop, calls=%fused_computation.12 | loop fusion | bytes 7340032 | tf_op jit(solution)/shard_map/slice | solution.py:14
  13.8 0.0 all-gather.13.cloned.1.call-update
  13.8 0.0 all-gather.9.cloned.1.call-start
  13.9 0.5 all-gather.9.cloned.1.call-update
  14.4 0.0 copy-done
  14.4 0.4 convert_reduce_fusion
  14.8 0.0 copy-done.1
  14.8 42.6 %all-gather.15.cloned.1.call-done = bf16[1,512,2048]{2,1,0:T(8,128)(2,1)} async-done(((bf16[1,128,2048]{2,1,0:T(8,128)(2,1)}), bf16[1,512,2048]{2,1,0:T(8,128)(2,1)}) %all-gather.15.cloned.1.call-update) | async-done | bytes 2097168 | tf_op jit(solution)/shard_map/all_gather | solution.py:11
  57.4 4.1 %bitcast_convert_fusion = f32[512,2048]{1,0:T(8,128)} fusion(bf16[1,512,2048]{2,1,0:T(8,128)(2,1)} %all-gather.15.cloned.1.call-done), kind=kLoop, calls=%fused_computation.6 | loop fusion | flops 1048576 | bytes 6291456 | tf_op jit(solution)/shard_map/convert_element_type | solution.py:18
  61.5 42.0 %all-gather.11.cloned.1.call-done = bf16[1,512,2048]{2,1,0:T(8,128)(2,1)} async-done(((bf16[1,128,2048]{2,1,0:T(8,128)(2,1)}), bf16[1,512,2048]{2,1,0:T(8,128)(2,1)}) %all-gather.11.cloned.1.call-update) | async-done | bytes 2097168 | tf_op jit(solution)/shard_map/all_gather | solution.py:11
  103.5 4.1 %bitcast_convert_fusion.1 = f32[512,2048]{1,0:T(8,128)} fusion(bf16[1,512,2048]{2,1,0:T(8,128)(2,1)} %all-gather.11.cloned.1.call-done), kind=kLoop, calls=%fused_computation.7 | loop fusion | flops 1048576 | bytes 6291456 | tf_op jit(solution)/shard_map/convert_element_type | solution.py:18
  107.6 48.6 %all-gather.13.cloned.1.call-done = bf16[1,512,7168]{2,1,0:T(8,128)(2,1)} async-done(((bf16[1,128,7168]{2,1,0:T(8,128)(2,1)}), bf16[1,512,7168]{2,1,0:T(8,128)(2,1)}) %all-gather.13.cloned.1.call-update) | async-done | bytes 7340048 | tf_op jit(solution)/shard_map/all_gather | solution.py:14
  156.2 39.0 %multiply_reduce_fusion = f32[512,2]{0,1:T(2,128)S(1)} fusion(f32[512,2048]{1,0:T(8,128)} %bitcast_convert_fusion, bf16[2,7168,2048]{2,1,0:T(8,128)(2,1)} %param.7, bf16[1,512,7168]{2,1,0:T(8,128)(2,1)} %all-gather.13.cloned.1.call-done), kind=kOutput, calls=%fused_computation | convolution fusion | flops 30068965376 | bytes 70258688 | tf_op jit(solution)/shard_map/to,qoi->tqi/dot_general | solution.py:12
  195.2 14.8 %all-gather.9.cloned.1.call-done = bf16[1,512,7168]{2,1,0:T(8,128)(2,1)} async-done(((bf16[1,128,7168]{2,1,0:T(8,128)(2,1)}), bf16[1,512,7168]{2,1,0:T(8,128)(2,1)}) %all-gather.9.cloned.1.call-update) | async-done | bytes 7340048 | tf_op jit(solution)/shard_map/all_gather | solution.py:14
  210.0 38.8 %multiply_reduce_fusion.1 = f32[512,2]{0,1:T(2,128)S(1)} fusion(f32[512,2048]{1,0:T(8,128)} %bitcast_convert_fusion.1, bf16[2,7168,2048]{2,1,0:T(8,128)(2,1)} %param.7, bf16[1,512,7168]{2,1,0:T(8,128)(2,1)} %all-gather.9.cloned.1.call-done), kind=kOutput, calls=%fused_computation.1 | convolution fusion | flops 30068965376 | bytes 70258688 | tf_op jit(solution)/shard_map/to,qoi->tqi/dot_general | solution.py:12
  248.8 33.8 %all-reduce = (f32[1,512,2]{1,0,2:T(1,128)S(1)}, f32[1,512,2]{1,0,2:T(1,128)S(1)}) all-reduce(f32[1,512,2]{1,0,2:T(1,128)S(1)} %stack.10, f32[1,512,2]{1,0,2:T(1,128)S(1)} %stack.9), channel_id=1, replica_groups=mesh['grp'=2,'inp'=4,'out'=4] {'inp','out'}, use_global_device_ids=true, to_apply=%region_3.0 | all-reduce | flops 2048 | bytes 16384 | tf_op jit(solution)/shard_map/psum | solution.py:19
  282.6 0.6 fusion.8
  (3 shorter events, 0.0 us)
Async XLA Ops:
  6.5 7.9 %copy-start = (s32[2,512]{1,0:T(2,128)S(1)}, s32[2,512]{1,0:T(2,128)}, u32[]{:S(2)}) copy-start(s32[2,512]{1,0:T(2,128)} %param.8) | copy-start | bytes 12292
  6.5 8.3 %copy-start.1 = (s32[2,512]{1,0:T(2,128)S(1)}, s32[2,512]{1,0:T(2,128)}, u32[]{:S(2)}) copy-start(s32[2,512]{1,0:T(2,128)} %param.9) | copy-start | bytes 12292
  6.5 50.9 %all-gather.15.cloned.1.call-start = ((), (), s32[]{:S(2)}) async-start(), calls=%async_computation.3 | async-start | bytes 2621440 | tf_op jit(solution)/shard_map/all_gather | solution.py:11
  8.9 94.6 %all-gather.11.cloned.1.call-start = ((), (), s32[]{:S(2)}) async-start(), calls=%async_computation.1 | async-start | bytes 2621440 | tf_op jit(solution)/shard_map/all_gather | solution.py:11
  9.6 146.6 %all-gather.13.cloned.1.call-start = ((), (), s32[]{:S(2)}) async-start(), calls=%async_computation.2 | async-start | bytes 9175040 | tf_op jit(solution)/shard_map/all_gather | solution.py:14
  13.8 196.1 %all-gather.9.cloned.1.call-start = ((), (), s32[]{:S(2)}) async-start(), calls=%async_computation | async-start | bytes 9175040 | tf_op jit(solution)/shard_map/all_gather | solution.py:14
Sparse Core Ops, SparseCore 0:
  9.0 48.3 all-gather.14
  59.0 44.4 all-gather.10
  105.0 51.1 all-gather.12
  157.6 52.2 all-gather.8
where the time goes:
time: 290 us
  waiting for transfers between devices  149 us (51%)
  matrix products  77.8 us (27%)
  blocking collectives  33.8 us (12%)
  between operations  13.2 us (5%)
  other arithmetic  9.25 us (3%)
  local copies, waits for them, and re-layouts  6.45 us (2%)
    all_gather x2, waiting for transfers between devices, shards(): gathered = lax.all_gather(activations[number], 'out', axis=0, tiled=True)  84.5 us
    dot_general x2, matrix products, shards(): jnp.einsum('to,qoi->tqi', lax.all_gather(out_grads[number], 'inp', axis=0...  77.8 us
    all_gather x2, waiting for transfers between devices, shards(): lax.all_gather(out_grads[number], 'inp', axis=0, tiled=True)  63.4 us
    psum x1, blocking collectives, shards(): partial_value = lax.psum(partial_value, ('inp', 'out'))  33.8 us
    convert_element_type x2, other arithmetic, shards(): gathered.astype(jnp.float32)[:, None, :]  8.22 us
  transfers between devices with their start and end apart: 4, of which 4 were waited for; matrix products, arithmetic and copies ran while one was open for 18% of the time, Pallas kernels for 0%

commit v1 on v0

v1 whole, which is shorter than its diff:
```python
import functools

import jax
import jax.numpy as jnp
from jax import lax
from jax.experimental import pallas as pl
from jax.experimental.pallas import tpu as pltpu
from jax.sharding import PartitionSpec as P

MESH = pl.DeviceIdType.MESH


def score_kernel(n_inp, n_out, chunk, width, g_ref, a_ref, q_ref, r_ref, gbuf, abuf, acc, qbuf, xin, xout,
                 own_sem, gsend, grecv, psend, precv, asend, arecv, qsem, isend, irecv, osend, orecv):
    chips = n_inp // 2
    me, z = lax.axis_index("inp"), lax.axis_index("out")
    y, core = me // 2, lax.rem(me, 2)
    partner = y * 2 + 1 - core
    nq, _, cols = q_ref.shape
    nb, tsh, feats = g_ref.shape
    atok = a_ref.shape[1]
    chunks = feats // chunk
    total = chips * chunks
    slots = qbuf.shape[0]
    rows = 2 * nb * tsh

    def remote(src, dst, send, recv, **where):
        return pltpu.make_async_remote_copy(
            src_ref=src, dst_ref=dst, send_sem=send, recv_sem=recv, device_id=where, device_id_type=MESH)

    def part_of(c):
        return g_ref.at[:, :, pl.ds(pl.multiple_of(c * chunk, chunk), chunk)]

    def own_copy(c):
        return pltpu.make_async_copy(part_of(c), gbuf.at[c, 0, core], own_sem.at[c])

    def far_copy(d, c):
        return remote(part_of(c), gbuf.at[c, d, core], gsend.at[d - 1, c], grecv.at[d - 1, c],
                      inp=lax.rem(y + chips - d, chips) * 2 + core)

    def near_copy(c):
        return remote(part_of(c), gbuf.at[c, 0, core], psend.at[0, c], precv.at[0, c], inp=partner)

    def pass_on(d, c):
        return remote(gbuf.at[c, d, core], gbuf.at[c, d, core], psend.at[d, c], precv.at[d, c], inp=partner)

    def rows_of(at):
        return pl.ds(pl.multiple_of(at * atok, atok), atok)

    def ring_copy(k):
        owner = lax.rem(z + n_out - (k - 1), n_out)
        src = a_ref if k == 1 else abuf.at[:, rows_of(owner), :]
        return remote(src, abuf.at[:, rows_of(owner), :], asend.at[k - 1], arecv.at[k - 1], out=lax.rem(z + 1, n_out))

    def q_copy(step):
        g, q = step // nq, lax.rem(step, nq)
        c = lax.rem(g, chunks)
        slot = lax.rem(step, slots)
        return pltpu.make_async_copy(
            q_ref.at[q, pl.ds(pl.multiple_of(c * chunk, chunk), chunk), :], qbuf.at[slot], qsem.at[slot])

    a_own = pltpu.make_async_copy(a_ref, abuf.at[:, rows_of(z), :], own_sem.at[chunks])
    a_own.start()
    for step in range(slots - 1):
        q_copy(jnp.int32(step)).start()
    for c in range(chunks):
        own_copy(c).start()

    barrier = pltpu.get_barrier_semaphore()
    for d in range(1, n_inp):
        pl.semaphore_signal(barrier, inc=1, device_id={"inp": lax.rem(me + d, n_inp)}, device_id_type=MESH)
    for d in range(1, n_out):
        pl.semaphore_signal(barrier, inc=1, device_id={"out": lax.rem(z + d, n_out)}, device_id_type=MESH)
    pl.semaphore_wait(barrier, n_inp + n_out - 2)

    for d in range(1, chips):
        for c in range(chunks):
            far_copy(d, c).start()
    ring_copy(1).start()
    for c in range(chunks):
        near_copy(c).start()

    def zero(i, _):
        acc[i // nq, lax.rem(i, nq)] = jnp.zeros((rows, cols), jnp.float32)
        return 0

    lax.fori_loop(0, chips * nq, zero, 0)

    def advance(g, _):
        p, c = g // chunks, lax.rem(g, chunks)

        @pl.when(p == 0)
        def _():
            own_copy(c).wait()
            near_copy(c).wait_recv()

        @pl.when(p > 0)
        def _():
            far_copy(p, c).wait_recv()
            pass_on(p, c).start()
            pass_on(p, c).wait_recv()

        for q in range(nq):
            step = g * nq + q

            @pl.when(step + slots - 1 < total * nq)
            def _():
                q_copy(step + slots - 1).start()

            q_copy(step).wait()
            slot = lax.rem(step, slots)

            def tile(n, _):
                at = pl.ds(pl.multiple_of(n * width, width), width)
                left = gbuf[c, p].reshape(rows, chunk)
                acc[p, q, :, at] += jnp.dot(left, qbuf[slot, :, at], preferred_element_type=jnp.float32)
                return 0

            lax.fori_loop(0, cols // width, tile, 0)
        return 0

    def finish(p, _):
        for k in range(2):
            shard = lax.rem(y + p, chips) * 2 + k
            for b in range(nb):
                act = abuf.at[b, pl.ds(pl.multiple_of(shard * tsh, tsh), tsh), :]
                top = (k * nb + b) * tsh
                for q in range(nq):
                    fold = jnp.zeros((tsh, 128), jnp.float32)
                    for n in range(cols // 128):
                        at = slice(n * 128, (n + 1) * 128)
                        fold += acc[p, q, top:top + tsh, at] * act[:, at].astype(jnp.float32)
                    xin[me, shard, q * nb + b, :] = jnp.sum(fold.T, axis=0)
        return 0

    at = 0
    for k in range(2, n_out):
        stop = min((k - 1) * 5, total - 1)
        lax.fori_loop(at, stop, advance, 0)
        at = stop
        ring_copy(k - 1).wait_recv()
        ring_copy(k).start()
    lax.fori_loop(at, total - 1, advance, 0)
    a_own.wait()
    if n_out > 1:
        ring_copy(n_out - 1).wait_recv()
    lax.fori_loop(0, chips - 1, finish, 0)
    lax.fori_loop(total - 1, total, advance, 0)
    finish(jnp.int32(chips - 1), 0)

    def in_copy(d):
        return remote(xin.at[me], xin.at[me], isend.at[d - 1], irecv.at[d - 1], inp=lax.rem(me + d, n_inp))

    def out_copy(d):
        return remote(xout.at[z], xout.at[z], osend.at[d - 1], orecv.at[d - 1], out=lax.rem(z + d, n_out))

    for d in range(1, n_inp):
        in_copy(d).start()
    for d in range(1, n_inp):
        in_copy(d).wait_recv()
    value = xin[0]
    for i in range(1, n_inp):
        value += xin[i]
    xout[z] = value
    for d in range(1, n_out):
        out_copy(d).start()
    for d in range(1, n_out):
        out_copy(d).wait_recv()
    value = xout[0]
    for i in range(1, n_out):
        value += xout[i]
    r_ref[...] = value

    for c in range(chunks):
        near_copy(c).wait_send()
        for d in range(1, chips):
            far_copy(d, c).wait_send()
            pass_on(d, c).wait_send()
    for k in range(1, n_out):
        ring_copy(k).wait_send()
        out_copy(k).wait_send()
    for d in range(1, n_inp):
        in_copy(d).wait_send()


def shards(n_inp, n_out, activations, out_grads, query_grads, token_ids, loss_mask):
    nb, tsh, feats = out_grads.shape
    nq, _, cols = query_grads.shape
    tokens = token_ids.shape[1]
    chips = n_inp // 2
    chunk = next(size for size in (1024, 512, 256, 128) if feats % size == 0)
    width = next(size for size in (512, 256, 128) if cols % size == 0)
    chunks = feats // chunk
    dma = pltpu.SemaphoreType.DMA
    raw = pl.pallas_call(
        functools.partial(score_kernel, n_inp, n_out, chunk, width),
        out_shape=jax.ShapeDtypeStruct((n_inp, nq * nb, tsh), jnp.float32),
        in_specs=[pl.BlockSpec(memory_space=pl.ANY)] * 3,
        out_specs=pl.BlockSpec(memory_space=pltpu.VMEM),
        scratch_shapes=[
            pltpu.VMEM((chunks, chips, 2, nb, tsh, chunk), jnp.bfloat16),
            pltpu.VMEM((nb, tokens, cols), jnp.bfloat16),
            pltpu.VMEM((chips, nq, 2 * nb * tsh, cols), jnp.float32),
            pltpu.VMEM((3, chunk, cols), jnp.bfloat16),
            pltpu.VMEM((n_inp, n_inp, nq * nb, tsh), jnp.float32),
            pltpu.VMEM((n_out, n_inp, nq * nb, tsh), jnp.float32),
            dma((chunks + 1,)),
            dma((max(chips - 1, 1), chunks)),
            dma((max(chips - 1, 1), chunks)),
            dma((chips, chunks)),
            dma((chips, chunks)),
            dma((max(n_out - 1, 1),)),
            dma((max(n_out - 1, 1),)),
            dma((3,)),
            dma((max(n_inp - 1, 1),)),
            dma((max(n_inp - 1, 1),)),
            dma((max(n_out - 1, 1),)),
            dma((max(n_out - 1, 1),)),
        ],
        compiler_params=pltpu.CompilerParams(
            collective_id=0, has_side_effects=True, vmem_limit_bytes=63 * 1024 * 1024),
    )(out_grads, activations, query_grads)
    equal = token_ids[:, :, None] == token_ids[:, None, :]
    counts = jnp.sum(equal.astype(jnp.int32), axis=2)
    weight = loss_mask.astype(jnp.float32) / counts.astype(jnp.float32)
    raw = jnp.transpose(raw.reshape(n_inp, nq, nb, tsh), (1, 2, 0, 3)).reshape(nq, nb, tokens)
    return raw * weight[None]


def solution(mesh):
    in_specs = (
        P("grp", "out", "inp"),
        P("grp", "inp", "out"),
        P(None, "out", "inp"),
        P("grp", None),
        P("grp", None),
    )
    body = functools.partial(shards, mesh.shape["inp"], mesh.shape["out"])
    return jax.shard_map(body, mesh=mesh, in_specs=in_specs, out_specs=P(None, "grp", None), check_vma=False)
```

time: 290 us -> 113 us (0.39)
  waiting for transfers between devices: 149 us -> 0 us
  Pallas kernels: 0 us -> 109 us
  matrix products: 77.8 us -> 0 us
  blocking collectives: 33.8 us -> 0 us
  between operations: 13.2 us -> 0.01 us
  local copies, waits for them, and re-layouts: 6.45 us -> 0 us
  other arithmetic: 9.25 us -> 3.15 us
    all_gather x4 -> x0, waiting for transfers between devices: 148 us -> none  [the longest x2 84.5 us: shards(): gathered = lax.all_gather(activations[number], 'out', axis=0, tiled=True)]
    pallas_call x0 -> x1, Pallas kernels: none -> 109 us  [shards(): pl.pallas_call(functools.partial(score_kernel, n_inp, n_out, chunk, width...]
    dot_general x2 -> x0, matrix products: 77.8 us -> none  [shards(): jnp.einsum('to,qoi->tqi', lax.all_gather(out_grads[number], 'inp', axis=0...]
    psum x1 -> x0, blocking collectives: 33.8 us -> none  [shards(): partial_value = lax.psum(partial_value, ('inp', 'out'))]
    convert_element_type x2 -> x0, other arithmetic: 8.22 us -> none  [shards(): gathered.astype(jnp.float32)[:, None, :]]
    slice x2 -> x0, local copies, waits for them, and re-layouts: 6.44 us -> none  [the longest x1 4.12 us: shards(): out_grads[number]]
  transfers between devices with their start and end apart: 4 -> 0, of which waited for: 4 -> 0; matrix products, arithmetic and copies ran while one was open for 18% -> 0% of each run, Pallas kernels for 0% -> 0%
where the time goes in v1:
time: 113 us; the launch traced here: 112 us
  Pallas kernels  109 us (96%)
  other arithmetic  3.15 us (3%)
    pallas_call x1, Pallas kernels, shards(): pl.pallas_call(functools.partial(score_kernel, n_inp, n_out, chunk, width...  109 us

profile of v1, /device:TPU:0, one launch (start us, length us, event | category | flops | bytes accessed | tf_op | source)
XLA Modules:
  0.0 112.4 jit_solution(7708845116690823233)
XLA Ops:
  0.0 1.1 %convert_reduce_fusion = s32[2,512]{1,0:T(2,128)S(1)} fusion(s32[2,512]{1,0:T(2,128)} %param.8), kind=kLoop, calls=%fused_computation | loop fusion | flops 1571840 | bytes 8192 | tf_op jit(solution)/shard_map/reduce_sum | solution.py:224
  1.1 0.7 convert_divide_fusion
  1.8 109.2 %shard_map.55 = f32[4,4,128]{2,1,0:T(4,128)} custom-call(bf16[2,128,7168]{2,1,0:T(8,128)(2,1)} %g_ref.1, bf16[2,128,2048]{2,1,0:T(8,128)(2,1)} %a_ref.1, bf16[2,7168,2048]{2,1,0:T(8,128)(2,1)} %q_ref.1), custom_call_target="tpu_custom_call" | custom-call | tf_op jit(solution)/shard_map/pallas_call | solution.py:195
  111.1 1.3 %bitcast_multiply_fusion = f32[2,2,512]{2,1,0:T(2,128)} fusion(f32[4,2,1,2,128]{4,3,2,1,0:T(2,128)} %bitcast.6, f32[2,512]{1,0:T(2,128)S(1)} %convert_divide_fusion), kind=kLoop, calls=%fused_computation.1 | loop fusion | flops 2048 | bytes 20480 | tf_op jit(solution)/shard_map/mul | solution.py:227

commit v2 on v1

--- a/solution.py
+++ b/solution.py
@@ -86,6 +86,39 @@
 
     lax.fori_loop(0, chips * nq, zero, 0)
 
+    def multiply(g, load, keep):
+        p, c = g // chunks, lax.rem(g, chunks)
+        for q in range(nq):
+            step = g * nq + q
+
+            if load:
+                @pl.when(step + slots - 1 < total * nq)
+                def _():
+                    q_copy(step + slots - 1).start()
+
+                q_copy(step).wait()
+            slot = lax.rem(step, slots)
+
+            def tile(n, _):
+                at = pl.ds(pl.multiple_of(n * width, width), width)
+                if keep is None:
+                    left = gbuf[c, p].reshape(rows, chunk)
+                    acc[p, q, :, at] += jnp.dot(left, qbuf[slot, :, at], preferred_element_type=jnp.float32)
+                else:
+                    half = pl.ds(pl.multiple_of(keep * (rows // 2), rows // 2), rows // 2)
+                    left = gbuf[c, p, keep].reshape(rows // 2, chunk)
+                    acc[p, q, half, at] += jnp.dot(left, qbuf[slot, :, at], preferred_element_type=jnp.float32)
+                return 0
+
+            lax.fori_loop(0, cols // width, tile, 0)
+
+            if load and q == 0:
+                @pl.when(jnp.logical_and(g + 1 >= chunks, g + 1 < total - 1))
+                def _():
+                    p_next, c_next = (g + 1) // chunks, lax.rem(g + 1, chunks)
+                    far_copy(p_next, c_next).wait_recv()
+                    pass_on(p_next, c_next).start()
+
     def advance(g, _):
         p, c = g // chunks, lax.rem(g, chunks)
 
@@ -96,28 +129,24 @@
 
         @pl.when(p > 0)
         def _():
+            pass_on(p, c).wait_recv()
+
+        multiply(g, True, None)
+        return 0
+
+    def last_chunk():
+        p, c = chips - 1, chunks - 1
+        g = jnp.int32(total - 1)
+        if p == 0:
+            own_copy(c).wait()
+            near_copy(c).wait_recv()
+            multiply(g, True, None)
+        else:
             far_copy(p, c).wait_recv()
             pass_on(p, c).start()
+            multiply(g, True, core)
             pass_on(p, c).wait_recv()
-
-        for q in range(nq):
-            step = g * nq + q
-
-            @pl.when(step + slots - 1 < total * nq)
-            def _():
-                q_copy(step + slots - 1).start()
-
-            q_copy(step).wait()
-            slot = lax.rem(step, slots)
-
-            def tile(n, _):
-                at = pl.ds(pl.multiple_of(n * width, width), width)
-                left = gbuf[c, p].reshape(rows, chunk)
-                acc[p, q, :, at] += jnp.dot(left, qbuf[slot, :, at], preferred_element_type=jnp.float32)
-                return 0
-
-            lax.fori_loop(0, cols // width, tile, 0)
-        return 0
+            multiply(g, False, 1 - core)
 
     def finish(p, _):
         for k in range(2):
@@ -145,7 +174,7 @@
     if n_out > 1:
         ring_copy(n_out - 1).wait_recv()
     lax.fori_loop(0, chips - 1, finish, 0)
-    lax.fori_loop(total - 1, total, advance, 0)
+    last_chunk()
     finish(jnp.int32(chips - 1), 0)
 
     def in_copy(d):
@@ -189,7 +218,7 @@
     tokens = token_ids.shape[1]
     chips = n_inp // 2
     chunk = next(size for size in (1024, 512, 256, 128) if feats % size == 0)
-    width = next(size for size in (512, 256, 128) if cols % size == 0)
+    width = next(size for size in (2048, 1024, 512, 256, 128) if cols % size == 0)
     chunks = feats // chunk
     dma = pltpu.SemaphoreType.DMA
     raw = pl.pallas_call(

time: 113 us -> 102 us (0.903)
  Pallas kernels: 109 us -> 98.7 us
    pallas_call x1, Pallas kernels: 109 us -> 98.7 us  [shards(): pl.pallas_call(functools.partial(score_kernel, n_inp, n_out, chunk, width...]
where the time goes in v2:
time: 102 us
  Pallas kernels  98.7 us (97%)
  other arithmetic  3.15 us (3%)
    pallas_call x1, Pallas kernels, shards(): pl.pallas_call(functools.partial(score_kernel, n_inp, n_out, chunk, width...  98.7 us

profile of v2, /device:TPU:0, one launch (start us, length us, event | category | flops | bytes accessed | tf_op | source)
XLA Modules:
  0.0 101.9 jit_solution(3305266495425286128)
XLA Ops:
  0.0 1.1 %convert_reduce_fusion = s32[2,512]{1,0:T(2,128)S(1)} fusion(s32[2,512]{1,0:T(2,128)} %param.8), kind=kLoop, calls=%fused_computation | loop fusion | flops 1571840 | bytes 8192 | tf_op jit(solution)/shard_map/reduce_sum | solution.py:253
  1.1 0.7 convert_divide_fusion
  1.8 98.7 %shard_map.55 = f32[4,4,128]{2,1,0:T(4,128)} custom-call(bf16[2,128,7168]{2,1,0:T(8,128)(2,1)} %g_ref.1, bf16[2,128,2048]{2,1,0:T(8,128)(2,1)} %a_ref.1, bf16[2,7168,2048]{2,1,0:T(8,128)(2,1)} %q_ref.1), custom_call_target="tpu_custom_call" | custom-call | tf_op jit(solution)/shard_map/pallas_call | solution.py:224
  100.6 1.3 %bitcast_multiply_fusion = f32[2,2,512]{2,1,0:T(2,128)} fusion(f32[4,2,1,2,128]{4,3,2,1,0:T(2,128)} %bitcast.6, f32[2,512]{1,0:T(2,128)S(1)} %convert_divide_fusion), kind=kLoop, calls=%fused_computation.1 | loop fusion | flops 2048 | bytes 20480 | tf_op jit(solution)/shard_map/mul | solution.py:256
